TPU v7x, 128 devices: a whole 4x4x4 slice. The times are simulated.
128 devices in a mesh: row: 8 (over y, core), col: 16 (over x, z).
Axes of the slice: x: 4, y: 4, z: 4, core: 2. Of those that a mesh axis runs over, the one named last changes fastest.
Arguments:
- theta: float32 [64, 256, 256], P('row', None, 'col'), may hold values from -6 to 6
- left_env: float32 [32, 32, 256, 256], P('row', 'col'), as said below
- right_env: float32 [8, 32, 256, 256], P(None, 'col'), as said below
- left_sector: int32 [64], replicated, may hold values from 0 to 31, as said below
- right_sector: int32 [64], P('row'), may hold values from 0 to 7
- term_on: int32 [64, 32], P('row', 'col'), may hold values 0 or 1
- left_size: int32 [32], replicated, may hold values from 1 to 256, 5120 in all
- right_size: int32 [8], replicated, may hold values from 1 to 256, 1280 in all
Outputs:
- new_theta: float32 [64, 256, 256], P('row', None, 'col')
- energy: float32 [], replicated
Inputs may be any that keep to these rules, and one draw needn't show every extreme that they name: `left_sector`: left sector s belongs to row s // 4. Block k belongs to row k // 8. The 8 blocks of one row name distinct left sectors; they name either none or exactly 2 sectors belonging to any one row, and the blocks of every row name 2 sectors belonging to one common row. `left_env`: each tile is symmetric in its last two dimensions. `right_env`: each tile is symmetric in its last two dimensions.
All inputs are finite; a program needn't handle non-finite values. No bound on the sum of `term_on` on one device may be relied on, other than what follows from the above.
Results may differ from a plain program's by a relative error of at most 0.0001.
Values sent between devices are 32-bit elements; how exact they have to be, the bound alone decides.
No kernel may reach another device: no remote copies, remote signals or barrier semaphores. Data moves between devices by JAX's collectives and lax.ppermute only.
A program may use at most 128 MiB of HBM per device.

v0:
```python
import jax
import jax.numpy as jnp
from jax import lax
from jax.sharding import Mesh, PartitionSpec as P

ITERS = 2
HALF = 128
COL = ("x", "z")
ALL = ("y", "c", "x", "z")
SWAP = [(0, 1), (1, 0)]
high = lax.Precision.HIGH


def grids():
    i = lax.broadcasted_iota(jnp.int32, (HALF, HALF), 0)
    j = lax.broadcasted_iota(jnp.int32, (HALF, HALF), 1)
    return (i, j)


def pack(tiles):
    i, j = grids()
    a00 = tiles[:, :HALF, :HALF]
    a01 = tiles[:, :HALF, HALF:]
    a11 = tiles[:, HALF:, HALF:]
    fold = jnp.where(i >= j, a00, a11)
    diag = jnp.sum(jnp.where(i == j, a11, 0.0), axis=1, keepdims=True)
    extra = jnp.pad(diag, ((0, 0), (0, 7), (0, HALF)))
    return jnp.concatenate([jnp.concatenate([fold, a01], axis=2), extra], axis=1)


def unpack(packed):
    i, j = grids()
    fold = packed[:, :HALF, :HALF]
    a01 = packed[:, :HALF, HALF:]
    diag = packed[:, HALF : HALF + 1, :HALF]
    flip = jnp.swapaxes(fold, 1, 2)
    a00 = jnp.where(i >= j, fold, flip)
    a11 = jnp.where(i == j, diag, jnp.where(i < j, fold, flip))
    top = jnp.concatenate([a00, a01], axis=2)
    low = jnp.concatenate([jnp.swapaxes(a01, 1, 2), a11], axis=2)
    return jnp.concatenate([top, low], axis=1)


def safe_div(value, norm):
    return jnp.where(norm > 0.0, value / jnp.where(norm > 0.0, norm, 1.0), 0.0)


def in_order(core, own, other):
    return jnp.where(core == 0, jnp.concatenate([own, other]), jnp.concatenate([other, own]))


def ritz_pair(stats):
    norm, a1, b1, a2, b2, a3 = [stats[:, m] for m in range(6)]

    def apply(x):
        return jnp.stack(
            [a1 * x[0] + b1 * x[1], b1 * x[0] + a2 * x[1] + b2 * x[2], b2 * x[1] + a3 * x[2]]
        )

    zero = jnp.zeros_like(norm)
    start = jnp.stack([norm, zero, zero])
    image = apply(start)
    norm_sq = jnp.sum(start * start)
    correlation = jnp.sum(start * image)
    inv_norm = 1.0 / jnp.sqrt(norm_sq)
    basis = start * inv_norm
    applied = image * inv_norm
    ritz = correlation / norm_sq
    for _ in range(ITERS):
        residual = applied - ritz * basis
        res_sq = jnp.sum(residual * residual)
        length = jnp.sqrt(res_sq)
        fresh = residual / length
        fresh_applied = apply(fresh)
        curvature = jnp.sum(fresh * fresh_applied)
        half_gap = 0.5 * (ritz - curvature)
        root = jnp.sqrt(half_gap * half_gap + res_sq)
        lowest = 0.5 * (ritz + curvature) - root
        first = curvature - lowest
        pair = jnp.sqrt(first * first + res_sq)
        basis = (first * basis - length * fresh) / pair
        applied = (first * applied - length * fresh_applied) / pair
        ritz = lowest
    return (basis, ritz)


def local(theta, left_env, right_env, left_sector, right_sector, term_on, left_size, right_size):
    plane = lax.axis_index("y")
    core = lax.axis_index("c")
    place = lax.axis_index(COL)
    tile = theta.shape[1]
    blocks = theta.shape[0]
    thin = jnp.swapaxes(theta, 1, 2)
    about = jnp.concatenate([right_sector[:, None], term_on], axis=1)
    about16 = in_order(core, about, lax.ppermute(about, "c", SWAP))
    thin16 = in_order(core, thin, lax.ppermute(thin, "c", SWAP))
    right16 = about16[:, 0]
    on16 = jnp.where(core == 0, about16[:, 1], about16[:, 2]).astype(jnp.float32)
    left16 = lax.dynamic_slice_in_dim(left_sector, plane * 16, 16)
    mine = pack(lax.dynamic_index_in_dim(left_env, core, 1, keepdims=False))
    theirs = pack(lax.dynamic_index_in_dim(left_env, 1 - core, 1, keepdims=False))
    eight = in_order(core, mine, lax.ppermute(theirs, "c", SWAP))
    every = lax.all_gather(eight, "y", axis=0, tiled=True)
    right_term = lax.dynamic_index_in_dim(right_env, core, 1, keepdims=False)
    right_slots = pack(jnp.take(right_term, right16, axis=0) * on16[:, None, None])
    slots = jnp.concatenate([right_slots, thin16], axis=1)
    arrived = lax.all_to_all(slots, COL, 0, 0, tiled=True)
    right = unpack(arrived[:, :136])
    block = arrived[:, 136:].reshape(tile, tile)
    left = unpack(lax.all_to_all(jnp.take(every, left16, axis=0), COL, 0, 0, tiled=True))
    live_left = left_size[left16[place]]
    live_right = right_size[right16[place]]
    at = lax.broadcasted_iota(jnp.int32, (tile, tile), 0)
    along = lax.broadcasted_iota(jnp.int32, (tile, tile), 1)
    mask = ((at < live_right) & (along < live_left)).astype(jnp.float32)

    def half_image(u):
        middle = jnp.einsum("wjb,bi->wji", right, u, precision=high)
        return jnp.einsum("wja,wai->ji", middle, left, precision=high)

    def operate(u):
        part = half_image(u)
        return (part + lax.ppermute(part, "c", SWAP)) * mask

    start = block * mask
    norm = jnp.sqrt(jnp.sum(start * start))
    q1 = safe_div(start, norm)
    h1 = operate(q1)
    a1 = jnp.sum(q1 * h1)
    w1 = h1 - a1 * q1
    w1 = w1 - jnp.sum(q1 * w1) * q1
    b1 = jnp.sqrt(jnp.sum(w1 * w1))
    q2 = safe_div(w1, b1)
    h2 = operate(q2)
    a2 = jnp.sum(q2 * h2)
    w2 = h2 - a2 * q2 - b1 * q1
    w2 = w2 - jnp.sum(q2 * w2) * q2 - jnp.sum(q1 * w2) * q1
    b2 = jnp.sqrt(jnp.sum(w2 * w2))
    q3 = safe_div(w2, b2)
    a3 = jnp.sum(q3 * half_image(q3))
    sent = jnp.where(core == 0, q2, q3).reshape(16, theta.shape[2], tile)
    got = lax.all_to_all(sent, COL, 0, 0, tiled=True)
    keep = lax.dynamic_slice_in_dim(got, core * blocks, blocks)
    give = lax.dynamic_slice_in_dim(got, (1 - core) * blocks, blocks)
    back = lax.ppermute(give, "c", SWAP)
    thin2 = jnp.where(core == 0, keep, back)
    thin3 = jnp.where(core == 0, back, keep)
    zero = jnp.float32(0.0)
    mine_stats = jnp.stack([norm, a1, b1, a2, b2, a3, zero, zero])
    stats = lax.all_to_all(jnp.broadcast_to(mine_stats, (128, 8)), ALL, 0, 0, tiled=True)
    stats = stats.reshape(4, 2, 16, 8)
    both = jnp.concatenate([stats[:, 0, :, :5], stats[:, 0, :, 5:] + stats[:, 1, :, 5:]], axis=2)
    both = both.reshape(64, 8)
    basis, ritz = ritz_pair(both)
    scale = jnp.sqrt(jnp.float32(64 * tile * tile))
    row = plane * 2 + core
    first = safe_div(basis[0], both[:, 0])
    coef = jnp.stack([first, basis[1], basis[2]]) * scale
    coef = lax.dynamic_slice_in_dim(coef, row * blocks, blocks, axis=1)
    own_left = lax.dynamic_slice_in_dim(left16, core * blocks, blocks)
    rows_live = left_size[own_left]
    cols_live = right_size[right_sector]
    cols = place * theta.shape[2] + lax.broadcasted_iota(jnp.int32, thin.shape, 1)
    rows = lax.broadcasted_iota(jnp.int32, thin.shape, 2)
    live = (cols < cols_live[:, None, None]) & (rows < rows_live[:, None, None])
    out = (
        coef[0][:, None, None] * jnp.where(live, thin, 0.0)
        + coef[1][:, None, None] * thin2
        + coef[2][:, None, None] * thin3
    )
    return (jnp.swapaxes(out, 1, 2), ritz)


def solution(mesh):
    fine = Mesh(mesh.devices.reshape(4, 2, 4, 4), ALL)
    row = ("y", "c")
    placed = (
        P(row, None, COL),
        P(row, COL, None, None),
        P(None, COL, None, None),
        P(),
        P(row),
        P(row, COL),
        P(),
        P(),
    )
    return jax.shard_map(
        local, mesh=fine, in_specs=placed, out_specs=(P(row, None, COL), P()), check_vma=False
    )
```

profile of v0, /device:TPU:1, one launch (start us, length us, event | category | flops | bytes accessed | tf_op | source)
XLA Modules:
  0.0 207.7 jit_solution(6810230765719790135)
XLA Ops:
  16.0 2.8 %gather_fusion = f32[16,256,256]{2,1,0:T(8,128)} fusion(f32[8,256,256]{2,1,0:T(8,128)S(1)} %dynamic-slice_bitcast_fusion, s32[1024]{0:T(1024)S(1)} %pad_clamp_fusion.3), kind=kCustom, calls=%fused_computation | custom fusion | bytes 8388672 | tf_op jit(solution)/shard_map/jit(_take)/gather | solution.py:105
  18.8 2.8 %select_multiply_fusion = f32[16,256,256]{2,1,0:T(8,128)S(1)} fusion(f32[16,256,256]{2,1,0:T(8,128)} %gather_fusion, f32[16]{0:T(128)S(1)} %get-tuple-element.64, pred[16]{0:T(512)(128)(4,1)S(1)} %and_bitcast_fusion), kind=kLoop, calls=%fused_computation.6 | loop fusion | flops 2097152 | bytes 8388688 | tf_op jit(solution)/shard_map/mul | solution.py:105
  23.6 7.7 %all-to-all-start = ((f32[16,152,256]{2,1,0:T(8,128)}), f32[16,152,256]{2,1,0:T(8,128)S(1)}, u32[]{:S(2)}, u32[]{:S(2)}) async-start(f32[16,152,256]{2,1,0:T(8,128)} %fusion), calls=%async_computation | async-start | bytes 4980736 | tf_op jit(solution)/shard_map/all_to_all | solution.py:107
  31.4 34.8 %all-gather.2.cloned.1.call-done = f32[32,136,256]{2,1,0:T(8,128)} async-done(((f32[8,136,256]{2,1,0:T(8,128)}), f32[32,136,256]{2,1,0:T(8,128)}) %all-gather.2.cloned.1.call-update) | async-done | bytes 4456464 | tf_op jit(solution)/shard_map/all_gather | solution.py:103
  66.2 4.4 %gather_fusion.1 = f32[16,136,256]{2,1,0:T(8,128)} fusion(f32[32,136,256]{2,1,0:T(8,128)} %all-gather.2.cloned.1.call-done, s32[1024]{0:T(1024)S(1)} %pad_clamp_fusion.2), kind=kCustom, calls=%fused_computation.1 | custom fusion | bytes 4456512 | tf_op jit(solution)/shard_map/jit(_take)/gather | solution.py:110
  70.6 3.3 %broadcast_select_fusion = f32[16,136,256]{2,1,0:T(8,128)} fusion(f32[16,136,256]{2,1,0:T(8,128)} %gather_fusion.1, pred[16]{0:T(512)(128)(4,1)S(1)} %get-tuple-element.20), kind=kLoop, calls=%fused_computation.18 | loop fusion | flops 557056 | bytes 4456464 | tf_op jit(solution)/shard_map/jit(_take)/select_n | solution.py:110
  74.0 6.7 %all-to-all-start.1 = ((f32[16,136,256]{2,1,0:T(8,128)}), f32[16,136,256]{2,1,0:T(8,128)}, u32[]{:S(2)}, u32[]{:S(2)}) async-start(f32[16,136,256]{2,1,0:T(8,128)} %broadcast_select_fusion), calls=%async_computation.1 | async-start | bytes 4456448 | tf_op jit(solution)/shard_map/all_to_all | solution.py:110
  91.5 2.5 %copy.54 = f32[16,128,128]{1,2,0:T(8,128)} copy(f32[16,128,128]{2,1,0:T(8,128)} %slice.189) | data formatting | bytes 2097152 | tf_op jit(solution)/shard_map/slice | solution.py:33
  94.1 16.2 %all-to-all-done.1 = f32[16,136,256]{2,1,0:T(8,128)} async-done(((f32[16,136,256]{2,1,0:T(8,128)}), f32[16,136,256]{2,1,0:T(8,128)}, u32[]{:S(2)}, u32[]{:S(2)}) %all-to-all-start.1) | async-done | bytes 2228256 | tf_op jit(solution)/shard_map/all_to_all | solution.py:110
  110.3 2.3 %slice.198 = f32[16,128,128]{2,1,0:T(8,128)} slice(f32[16,136,256]{2,1,0:T(8,128)} %all-to-all-done.1), slice={[0:16], [0:128], [0:128]} | slice | bytes 2097152 | tf_op jit(solution)/shard_map/slice | solution.py:33
  112.7 2.6 %copy.66 = f32[16,128,128]{1,2,0:T(8,128)} copy(f32[16,128,128]{2,1,0:T(8,128)} %slice.198) | data formatting | bytes 2097152
  116.1 5.4 %bitcast_select_fusion.1 = (f32[16,128,128]{2,1,0:T(8,128)}, f32[16,128,128]{2,1,0:T(8,128)}, f32[16,128,128]{2,1,0:T(8,128)}, f32[16,128,128]{2,1,0:T(8,128)}, ...) fusion(f32[16,128,128]{1,2,0:T(8,128)} %copy.66, ...), kind=kLoop, calls=%fused_computation.21 | loop fusion | flops 1572864 | bytes 13697024 | tf_op jit(solution)/shard_map/jit(_where)/select_n | solution.py:37
  123.1 2.5 %copy.67 = f32[16,128,128]{1,2,0:T(8,128)} copy(f32[16,128,128]{2,1,0:T(8,128)} %get-tuple-element.33) | data formatting | bytes 2097152
  125.7 3.6 %fusion.7 = f32[16,256,256]{2,1,0:T(8,128)S(1)} fusion(f32[16,128,128]{2,1,0:T(8,128)} %get-tuple-element.46, f32[16,128,128]{2,1,0:T(8,128)S(1)} %copy.56, f32[16,128,128]{2,1,0:T(8,128)S(1)} %copy-done.2, f32[16,128,128]{2,1,0:T(8,128)} %get-tuple-element.47, f32[256,256]{1,0:T(8,128)S(1)} %fusion.10), kind=kOutput, calls=%fused_computation.31 | convolution fusion | flops 1613758464 | bytes 8650752 | tf_op jit(solution)/shard_map/wjb,bi->wji/dot_general | solution.py:118
  129.4 2.2 %convolution_bitcast_fusion.2 = f32[256,256]{1,0:T(8,128)S(1)} fusion(f32[16,256,256]{2,1,0:T(8,128)S(1)} %fusion.7, f32[16,128,128]{2,1,0:T(8,128)S(1)} %copy-done.12, f32[16,128,128]{2,1,0:T(8,128)S(1)} %bitcast.176, f32[16,128,128]{2,1,0:T(8,128)S(1)} %copy-done.3, f32[16,128,128]{2,1,0:T(8,128)S(1)} %copy-done.9), kind=kOutput, calls=%fused_computation.15 | convolution fusion | flops 1613758464 | bytes 8650752 | tf_op jit(solution)/shard_map/wja,wai->ji/dot_general | solution.py:119
  131.5 3.6 %collective-permute-start.3 = (f32[256,256]{1,0:T(8,128)S(1)}, f32[256,256]{1,0:T(8,128)S(1)}, u32[]{:S(2)}, u32[]{:S(2)}) collective-permute-start(f32[256,256]{1,0:T(8,128)S(1)} %convolution_bitcast_fusion.2), channel_id=1, source_target_pairs={{0,16},{16,0},{1,17},{17,1},{2,18},{18,2},{3,19},{19,3},{4,20},{20... | collective-permute-start | bytes 786440 | tf_op jit(solution)/shard_map/ppermute | solution.py:123
  142.7 3.6 %fusion.6 = f32[16,256,256]{2,1,0:T(8,128)S(1)} fusion(f32[16,128,128]{2,1,0:T(8,128)} %get-tuple-element.46, f32[16,128,128]{2,1,0:T(8,128)S(1)} %copy.56, f32[16,128,128]{2,1,0:T(8,128)S(1)} %copy-done.2, f32[16,128,128]{2,1,0:T(8,128)} %get-tuple-element.47, f32[256,256]{1,0:T(8,128)S(1)} %divide_select_fusion.1), kind=kOutput, calls=%fused_computation.30 | convolution fusion | flops 1613758464 | bytes 8650752 | tf_op jit(solution)/shard_map/wjb,bi->wji/dot_general | solution.py:118
  146.4 2.2 %convolution_bitcast_fusion.1 = f32[256,256]{1,0:T(8,128)S(1)} fusion(f32[16,256,256]{2,1,0:T(8,128)S(1)} %fusion.6, f32[16,128,128]{2,1,0:T(8,128)S(1)} %copy-done.13, f32[16,128,128]{2,1,0:T(8,128)S(1)} %bitcast.177, f32[16,128,128]{2,1,0:T(8,128)S(1)} %copy-done.4, f32[16,128,128]{2,1,0:T(8,128)S(1)} %copy-done.10), kind=kOutput, calls=%fused_computation.14 | convolution fusion | flops 1613758464 | bytes 8650752 | tf_op jit(solution)/shard_map/wja,wai->ji/dot_general | solution.py:119
  152.5 2.7 %multiply_reduce_fusion = (f32[]{:T(128)}, f32[256,256]{1,0:T(8,128)S(1)}) fusion(f32[]{:T(128)} %get-tuple-element.7, f32[256,256]{1,0:T(8,128)S(1)} %divide_select_fusion.1, f32[]{:T(128)} %get-tuple-element.6, f32[]{:T(128)} %sqrt.31, f32[256,256]{1,0:T(8,128)S(1)} %get-tuple-element.17, f32[]{:T(128)} %get-tuple-element.16, f32[]{:T(128)S(6)} %select_n.228, ...), kind=kLoop, calls=%fused_computation.47 | loop fusion | flops 917503 | bytes 1049113 | tf_op jit(solution)/shard_map/reduce_sum | solution.py:138
  155.8 3.6 %fusion.5 = f32[16,256,256]{2,1,0:T(8,128)S(1)} fusion(f32[16,128,128]{2,1,0:T(8,128)} %get-tuple-element.46, f32[16,128,128]{2,1,0:T(8,128)S(1)} %copy.56, f32[16,128,128]{2,1,0:T(8,128)S(1)} %copy-done.2, f32[16,128,128]{2,1,0:T(8,128)} %get-tuple-element.47, f32[256,256]{1,0:T(8,128)S(1)} %get-tuple-element.15, f32[]{:T(128)S(6)} %select_n.249, pred[]{:T(512)S(6)} %gt.28), kind=kOutput, calls=%fused_computation.29 | convolution fusion | flops 1613889536 | bytes 8650757 | tf_op jit(solution)/shard_map/wjb,bi->wji/dot_general | solution.py:118
  159.5 2.8 %fusion.8 = f32[]{:T(128)} fusion(f32[16,256,256]{2,1,0:T(8,128)S(1)} %fusion.5, f32[16,128,128]{2,1,0:T(8,128)S(1)} %copy-done.14, f32[16,128,128]{2,1,0:T(8,128)S(1)} %bitcast.178, f32[16,128,128]{2,1,0:T(8,128)S(1)} %copy-done.5, f32[16,128,128]{2,1,0:T(8,128)S(1)} %copy-done.11, f32[256,256]{1,0:T(8,128)S(1)} %get-tuple-element.15, f32[]{:T(128)S(6)} %select_n.249, ...), kind=kOutput, calls=%fused_computation.32 | convolution fusion | flops 1614020608 | bytes 8650761 | tf_op jit(solution)/shard_map/wja,wai->ji/dot_general | solution.py:119
  164.7 4.8 %all-to-all-start.2 = ((f32[128,1,8]{2,1,0:T(1,128)}), f32[128,1,8]{2,1,0:T(1,128)S(1)}, u32[]{:S(2)}, u32[]{:S(2)}) async-start(f32[128,1,8]{2,1,0:T(1,128)} %broadcast_in_dim.146), calls=%async_computation.2 | async-start | bytes 131072 | tf_op jit(solution)/shard_map/all_to_all | solution.py:150
  170.3 8.7 %all-to-all-done.2 = f32[128,1,8]{2,1,0:T(1,128)S(1)} async-done(((f32[128,1,8]{2,1,0:T(1,128)}), f32[128,1,8]{2,1,0:T(1,128)S(1)}, u32[]{:S(2)}, u32[]{:S(2)}) %all-to-all-start.2) | async-done | bytes 4128 | tf_op jit(solution)/shard_map/all_to_all | solution.py:150
  179.0 3.5 %all-to-all-start.3 = ((f32[16,16,256]{2,1,0:T(8,128)}), f32[16,16,256]{2,1,0:T(8,128)S(1)}, u32[]{:S(2)}, u32[]{:S(2)}) async-start(f32[16,16,256]{2,1,0:T(8,128)} %bitcast.44), calls=%async_computation.3 | async-start | bytes 524288 | tf_op jit(solution)/shard_map/all_to_all | solution.py:142
  (130 shorter events, 40.5 us)
Async XLA Ops:
  7.2 59.1 %all-gather.2.cloned.1.call-start = ((), (), s32[]{:S(2)}) async-start(), calls=%async_computation.4 | async-start | bytes 5570560 | tf_op jit(solution)/shard_map/all_gather | solution.py:103
  8.9 4.5 %copy-start.16 = (s32[8,2]{0,1:T(2,128)S(1)}, s32[8,2]{0,1:T(2,128)}, u32[]{:S(2)}) copy-start(s32[8,2]{0,1:T(2,128)} %param.13) | copy-start | bytes 196
  9.0 4.5 %copy-start.17 = (s32[8]{0:T(128)S(1)}, s32[8]{0:T(128)}, u32[]{:S(2)}) copy-start(s32[8]{0:T(128)} %param.12) | copy-start | bytes 100
  9.0 5.0 %copy-start.15 = (f32[8,256,16]{1,2,0:T(8,128)S(1)}, f32[8,256,16]{1,2,0:T(8,128)}, u32[]{:S(2)}) copy-start(f32[8,256,16]{1,2,0:T(8,128)} %param.8) | copy-start | bytes 393220
  9.2 3.1 %collective-permute-start.2 = (f32[4,136,256]{2,1,0:T(8,128)S(1)}, f32[4,136,256]{2,1,0:T(8,128)S(1)}, u32[]{:S(2)}, u32[]{:S(2)}) collective-permute-start(f32[4,136,256]{2,1,0:T(8,128)S(1)} %select_maximum_fusion.1), channel_id=1, source_target_pairs={{0,16},{16,0},{1,17},{17,1},{2,18},{18,2},{3,19},{19,3},{4,20},{20... | collective-permute-start | bytes 1671176 | tf_op jit(solution)/shard_map/ppermute | solution.py:102
  13.5 2.4 %collective-permute-start = (s32[8,3]{0,1:T(4,128)S(1)}, s32[8,3]{0,1:T(4,128)S(1)}, u32[]{:S(2)}, u32[]{:S(2)}) collective-permute-start(s32[8,3]{0,1:T(4,128)S(1)} %pad_add_fusion), channel_id=1, source_target_pairs={{0,16},{16,0},{1,17},{17,1},{2,18},{18,2},{3,19},{19,3},{4,20},{20... | collective-permute-start | bytes 296 | tf_op jit(solution)/shard_map/ppermute | solution.py:95
  13.9 7.9 %collective-permute-start.1 = (f32[8,16,256]{2,1,0:T(8,128)S(1)}, f32[8,16,256]{2,1,0:T(8,128)S(1)}, u32[]{:S(2)}, u32[]{:S(2)}) collective-permute-start(f32[8,16,256]{2,1,0:T(8,128)S(1)} %bitcast.179), channel_id=1, source_target_pairs={{0,16},{16,0},{1,17},{17,1},{2,18},{18,2},{3,19},{19,3},{4,20},{20... | collective-permute-start | bytes 393224 | tf_op jit(solution)/shard_map/ppermute | solution.py:96
  21.9 9.4 %copy-start.18 = (s32[64]{0:T(128)S(1)}, s32[64]{0:T(128)}, u32[]{:S(2)}) copy-start(s32[64]{0:T(128)} %param.11) | copy-start | bytes 772
  23.6 50.4 %all-to-all-start = ((f32[16,152,256]{2,1,0:T(8,128)}), f32[16,152,256]{2,1,0:T(8,128)S(1)}, u32[]{:S(2)}, u32[]{:S(2)}) async-start(f32[16,152,256]{2,1,0:T(8,128)} %fusion), calls=%async_computation | async-start | bytes 4980736 | tf_op jit(solution)/shard_map/all_to_all | solution.py:107
  70.6 12.6 %copy-start = (s32[32]{0:T(128)S(1)}, s32[32]{0:T(128)}, u32[]{:S(2)}) copy-start(s32[32]{0:T(128)} %param.14) | copy-start | bytes 388
  70.6 15.8 %copy-start.1 = (s32[8]{0:T(128)S(1)}, s32[8]{0:T(128)}, u32[]{:S(2)}) copy-start(s32[8]{0:T(128)} %param.15) | copy-start | bytes 100
  74.0 36.4 %all-to-all-start.1 = ((f32[16,136,256]{2,1,0:T(8,128)}), f32[16,136,256]{2,1,0:T(8,128)}, u32[]{:S(2)}, u32[]{:S(2)}) async-start(f32[16,136,256]{2,1,0:T(8,128)} %broadcast_select_fusion), calls=%async_computation.1 | async-start | bytes 4456448 | tf_op jit(solution)/shard_map/all_to_all | solution.py:110
  121.5 4.2 %copy-start.2 = (f32[16,128,128]{2,1,0:T(8,128)S(1)}, f32[16,128,128]{2,1,0:T(8,128)}, u32[]{:S(2)}) copy-start(f32[16,128,128]{2,1,0:T(8,128)} %get-tuple-element.44) | copy-start | bytes 3145732
  125.7 3.7 %copy-start.9 = (f32[16,128,128]{2,1,0:T(8,128)S(1)}, f32[16,128,128]{2,1,0:T(8,128)}, u32[]{:S(2)}) copy-start(f32[16,128,128]{2,1,0:T(8,128)} %get-tuple-element.27) | copy-start | bytes 3145732
  125.7 3.7 %copy-start.12 = (f32[16,128,128]{2,1,0:T(8,128)S(1)}, f32[16,128,128]{2,1,0:T(8,128)}, u32[]{:S(2)}) copy-start(f32[16,128,128]{2,1,0:T(8,128)} %get-tuple-element.28) | copy-start | bytes 3145732
  131.5 4.8 %collective-permute-start.3 = (f32[256,256]{1,0:T(8,128)S(1)}, f32[256,256]{1,0:T(8,128)S(1)}, u32[]{:S(2)}, u32[]{:S(2)}) collective-permute-start(f32[256,256]{1,0:T(8,128)S(1)} %convolution_bitcast_fusion.2), channel_id=1, source_target_pairs={{0,16},{16,0},{1,17},{17,1},{2,18},{18,2},{3,19},{19,3},{4,20},{20... | collective-permute-start | bytes 786440 | tf_op jit(solution)/shard_map/ppermute | solution.py:123
  142.7 3.7 %copy-start.4 = (f32[16,128,128]{2,1,0:T(8,128)S(1)}, f32[16,128,128]{2,1,0:T(8,128)}, u32[]{:S(2)}) copy-start(f32[16,128,128]{2,1,0:T(8,128)} %get-tuple-element.33) | copy-start | bytes 3145732
  142.7 3.7 %copy-start.7 = (f32[16,128,128]{1,2,0:T(8,128)S(1)}, f32[16,128,128]{1,2,0:T(8,128)}, u32[]{:S(2)}) copy-start(f32[16,128,128]{1,2,0:T(8,128)} %copy.67) | copy-start | bytes 3145732
  142.7 3.7 %copy-start.10 = (f32[16,128,128]{2,1,0:T(8,128)S(1)}, f32[16,128,128]{2,1,0:T(8,128)}, u32[]{:S(2)}) copy-start(f32[16,128,128]{2,1,0:T(8,128)} %get-tuple-element.27) | copy-start | bytes 3145732
  142.7 3.7 %copy-start.13 = (f32[16,128,128]{2,1,0:T(8,128)S(1)}, f32[16,128,128]{2,1,0:T(8,128)}, u32[]{:S(2)}) copy-start(f32[16,128,128]{2,1,0:T(8,128)} %get-tuple-element.28) | copy-start | bytes 3145732
  148.6 1.8 collective-permute-start.4
  164.7 14.3 %all-to-all-start.2 = ((f32[128,1,8]{2,1,0:T(1,128)}), f32[128,1,8]{2,1,0:T(1,128)S(1)}, u32[]{:S(2)}, u32[]{:S(2)}) async-start(f32[128,1,8]{2,1,0:T(1,128)} %broadcast_in_dim.146), calls=%async_computation.2 | async-start | bytes 131072 | tf_op jit(solution)/shard_map/all_to_all | solution.py:150
  179.0 17.8 %all-to-all-start.3 = ((f32[16,16,256]{2,1,0:T(8,128)}), f32[16,16,256]{2,1,0:T(8,128)S(1)}, u32[]{:S(2)}, u32[]{:S(2)}) async-start(f32[16,16,256]{2,1,0:T(8,128)} %bitcast.44), calls=%async_computation.3 | async-start | bytes 524288 | tf_op jit(solution)/shard_map/all_to_all | solution.py:142
  196.8 2.1 %collective-permute-start.5 = (f32[8,16,256]{2,1,0:T(8,128)S(1)}, f32[8,16,256]{2,1,0:T(8,128)S(1)}, u32[]{:S(2)}, u32[]{:S(2)}) collective-permute-start(f32[8,16,256]{2,1,0:T(8,128)S(1)} %constant_dynamic-slice_fusion), channel_id=1, source_target_pairs={{0,16},{16,0},{1,17},{17,1},{2,18},{18,2},{3,19},{19,3},{4,20},{20... | collective-permute-start | bytes 393224 | tf_op jit(solution)/shard_map/ppermute | solution.py:145
  (6 other events, 21.8 us)
Sparse Core Ops, SparseCore 0:
  13.6 52.6 all-gather.1
where the time goes:
time: 209 us; the launch traced here: 208 us
  waiting for transfers between devices  63.4 us (30%)
  other arithmetic  33 us (16%)
  between operations  31.8 us (15%)
  local copies, waits for them, and re-layouts  31.4 us (15%)
  starting transfers between devices  30 us (14%)
  matrix products  18 us (9%)
    all_gather x1, waiting for transfers between devices, local(): every = lax.all_gather(eight, 'y', axis=0, tiled=True)  34.8 us
    all_to_all x1, waiting for transfers between devices, local(): lax.all_to_all(jnp.take(every, left16, axis=0), COL, 0, 0, tiled=True)  16.2 us
    dot_general x3, matrix products, half_image(): middle = jnp.einsum('wjb,bi->wji', right, u, precision=high)  10.8 us
    all_to_all x1, waiting for transfers between devices, local(): lax.all_to_all(jnp.broadcast_to(mine_stats, (128, 8)), ALL, 0, 0, tiled=T...  8.72 us
    all_to_all x1, starting transfers between devices, local(): arrived = lax.all_to_all(slots, COL, 0, 0, tiled=True)  7.68 us
    dot_general x3, matrix products, half_image(): return jnp.einsum('wja,wai->ji', middle, left, precision=high)  7.13 us
    all_to_all x1, starting transfers between devices, local(): lax.all_to_all(jnp.take(every, left16, axis=0), COL, 0, 0, tiled=True)  6.71 us
    slice x3, local copies, waits for them, and re-layouts, unpack(): fold = packed[:, :HALF, :HALF]  5.98 us
  transfers between devices with their start and end apart: 11, of which 6 were waited for; matrix products, arithmetic and copies ran while one was open for 16% of the time, Pallas kernels for 0%

commit v1 on v0

--- a/solution.py
+++ b/solution.py
@@ -100,7 +100,9 @@
     mine = pack(lax.dynamic_index_in_dim(left_env, core, 1, keepdims=False))
     theirs = pack(lax.dynamic_index_in_dim(left_env, 1 - core, 1, keepdims=False))
     eight = in_order(core, mine, lax.ppermute(theirs, "c", SWAP))
-    every = lax.all_gather(eight, "y", axis=0, tiled=True)
+    every = jnp.concatenate(
+        lax.all_to_all(jnp.stack([eight] * lax.axis_size("y")), "y", 0, 0), axis=0
+    )
     right_term = lax.dynamic_index_in_dim(right_env, core, 1, keepdims=False)
     right_slots = pack(jnp.take(right_term, right16, axis=0) * on16[:, None, None])
     slots = jnp.concatenate([right_slots, thin16], axis=1)

time: 209 us -> 231 us (1.11)
  waiting for transfers between devices: 63.4 us -> 89.2 us
  between operations: 31.8 us -> 18.3 us
  starting transfers between devices: 30 us -> 37.2 us
  local copies, waits for them, and re-layouts: 31.4 us -> 34.2 us
    all_to_all x0 -> x1, waiting for transfers between devices: none -> 41.4 us  [local(): lax.all_to_all(jnp.stack([eight] * lax.axis_size('y')), 'y', 0, 0)]
    all_gather x1 -> x0, waiting for transfers between devices: 34.8 us -> none  [local(): every = lax.all_gather(eight, 'y', axis=0, tiled=True)]
    all_to_all x1, waiting for transfers between devices: 0.01 us -> 22.7 us  [local(): arrived = lax.all_to_all(slots, COL, 0, 0, tiled=True)]
    all_to_all x0 -> x1, starting transfers between devices: none -> 5.02 us  [local(): lax.all_to_all(jnp.stack([eight] * lax.axis_size('y')), 'y', 0, 0)]
    all_to_all x1, waiting for transfers between devices: 16.2 us -> 12.8 us  [local(): lax.all_to_all(jnp.take(every, left16, axis=0), COL, 0, 0, tiled=True)]
    ppermute x2, starting transfers between devices: 4.04 us -> 7.25 us  [operate(): return (part + lax.ppermute(part, 'c', SWAP)) * mask]
    another operation x1 -> x2, local copies, waits for them, and re-layouts: 0.01 us -> 2.48 us  [the longest x1 2.48 us: local(): jnp.stack([eight] * lax.axis_size('y'))]
  transfers between devices with their start and end apart: 11 -> 11, of which waited for: 6 -> 7; matrix products, arithmetic and copies ran while one was open for 16% -> 14% of each run, Pallas kernels for 0% -> 0%
where the time goes in v1:
time: 231 us; the launch traced here: 229 us
  waiting for transfers between devices  89.2 us (39%)
  starting transfers between devices  37.2 us (16%)
  local copies, waits for them, and re-layouts  34.2 us (15%)
  other arithmetic  32.5 us (14%)
  between operations  18.3 us (8%)
  matrix products  18 us (8%)
    all_to_all x1, waiting for transfers between devices, local(): lax.all_to_all(jnp.stack([eight] * lax.axis_size('y')), 'y', 0, 0)  41.4 us
    all_to_all x1, waiting for transfers between devices, local(): arrived = lax.all_to_all(slots, COL, 0, 0, tiled=True)  22.7 us
    all_to_all x1, waiting for transfers between devices, local(): lax.all_to_all(jnp.take(every, left16, axis=0), COL, 0, 0, tiled=True)  12.8 us
    dot_general x3, matrix products, half_image(): middle = jnp.einsum('wjb,bi->wji', right, u, precision=high)  10.8 us
    all_to_all x1, waiting for transfers between devices, local(): lax.all_to_all(jnp.broadcast_to(mine_stats, (128, 8)), ALL, 0, 0, tiled=T...  8.72 us
    all_to_all x1, starting transfers between devices, local(): arrived = lax.all_to_all(slots, COL, 0, 0, tiled=True)  7.58 us
    ppermute x2, starting transfers between devices, operate(): return (part + lax.ppermute(part, 'c', SWAP)) * mask  7.25 us
    dot_general x3, matrix products, half_image(): return jnp.einsum('wja,wai->ji', middle, left, precision=high)  7.21 us
  transfers between devices with their start and end apart: 11, of which 7 were waited for; matrix products, arithmetic and copies ran while one was open for 14% of the time, Pallas kernels for 0%

profile of v1, /device:TPU:1, one launch (start us, length us, event | category | flops | bytes accessed | tf_op | source)
XLA Modules:
  0.0 229.5 jit_solution(2158344535686885161)
XLA Ops:
  5.7 2.5 %stack.56 = f32[4,8,136,256]{3,2,1,0:T(8,128)} broadcast(f32[8,136,256]{2,1,0:T(8,128)S(1)} %maximum_select_fusion), dimensions={1,2,3} | broadcast | bytes 5570560 | tf_op jit(solution)/shard_map/stack | solution.py:104
  8.2 5.0 %all-to-all-start.1 = ((f32[4,8,136,256]{3,2,1,0:T(8,128)}), f32[4,8,136,256]{3,2,1,0:T(8,128)}, u32[]{:S(2)}, u32[]{:S(2)}) async-start(f32[4,8,136,256]{3,2,1,0:T(8,128)} %stack.56), calls=%async_computation.1 | async-start | bytes 8912896 | tf_op jit(solution)/shard_map/all_to_all | solution.py:104
  15.8 2.8 %gather_fusion = f32[16,256,256]{2,1,0:T(8,128)} fusion(f32[8,256,256]{2,1,0:T(8,128)S(1)} %dynamic-slice_bitcast_fusion, s32[1024]{0:T(1024)S(1)} %pad_clamp_fusion.3), kind=kCustom, calls=%fused_computation | custom fusion | bytes 8388672 | tf_op jit(solution)/shard_map/jit(_take)/gather | solution.py:107
  18.6 2.8 %select_multiply_fusion = f32[16,256,256]{2,1,0:T(8,128)S(1)} fusion(f32[16,256,256]{2,1,0:T(8,128)} %gather_fusion, f32[16]{0:T(128)S(1)} %get-tuple-element.64, pred[16]{0:T(512)(128)(4,1)S(1)} %and_bitcast_fusion), kind=kLoop, calls=%fused_computation.6 | loop fusion | flops 2097152 | bytes 8388688 | tf_op jit(solution)/shard_map/mul | solution.py:107
  23.4 41.4 %all-to-all-done.1 = f32[4,8,136,256]{3,2,1,0:T(8,128)} async-done(((f32[4,8,136,256]{3,2,1,0:T(8,128)}), f32[4,8,136,256]{3,2,1,0:T(8,128)}, u32[]{:S(2)}, u32[]{:S(2)}) %all-to-all-start.1) | async-done | bytes 4456480 | tf_op jit(solution)/shard_map/all_to_all | solution.py:104
  64.8 7.6 %all-to-all-start = ((f32[16,152,256]{2,1,0:T(8,128)}), f32[16,152,256]{2,1,0:T(8,128)S(1)}, u32[]{:S(2)}, u32[]{:S(2)}) async-start(f32[16,152,256]{2,1,0:T(8,128)} %fusion), calls=%async_computation | async-start | bytes 4980736 | tf_op jit(solution)/shard_map/all_to_all | solution.py:109
  72.4 4.3 %gather_fusion.1 = f32[16,136,256]{2,1,0:T(8,128)} fusion(f32[32,136,256]{2,1,0:T(8,128)} %bitcast.22, s32[1024]{0:T(1024)S(1)} %pad_clamp_fusion.2), kind=kCustom, calls=%fused_computation.1 | custom fusion | bytes 4456512 | tf_op jit(solution)/shard_map/jit(_take)/gather | solution.py:112
  76.8 3.3 %broadcast_select_fusion = f32[16,136,256]{2,1,0:T(8,128)} fusion(f32[16,136,256]{2,1,0:T(8,128)} %gather_fusion.1, pred[16]{0:T(512)(128)(4,1)S(1)} %get-tuple-element.20), kind=kLoop, calls=%fused_computation.18 | loop fusion | flops 557056 | bytes 4456464 | tf_op jit(solution)/shard_map/jit(_take)/select_n | solution.py:112
  80.1 22.7 %all-to-all-done = f32[16,152,256]{2,1,0:T(8,128)S(1)} async-done(((f32[16,152,256]{2,1,0:T(8,128)}), f32[16,152,256]{2,1,0:T(8,128)S(1)}, u32[]{:S(2)}, u32[]{:S(2)}) %all-to-all-start) | async-done | bytes 2490400 | tf_op jit(solution)/shard_map/all_to_all | solution.py:109
  102.8 5.5 %all-to-all-start.2 = ((f32[16,136,256]{2,1,0:T(8,128)}), f32[16,136,256]{2,1,0:T(8,128)}, u32[]{:S(2)}, u32[]{:S(2)}) async-start(f32[16,136,256]{2,1,0:T(8,128)} %broadcast_select_fusion), calls=%async_computation.2 | async-start | bytes 4456448 | tf_op jit(solution)/shard_map/all_to_all | solution.py:112
  119.1 2.6 %copy.54 = f32[16,128,128]{1,2,0:T(8,128)} copy(f32[16,128,128]{2,1,0:T(8,128)} %slice.189) | data formatting | bytes 2097152 | tf_op jit(solution)/shard_map/slice | solution.py:33
  121.8 12.8 %all-to-all-done.2 = f32[16,136,256]{2,1,0:T(8,128)} async-done(((f32[16,136,256]{2,1,0:T(8,128)}), f32[16,136,256]{2,1,0:T(8,128)}, u32[]{:S(2)}, u32[]{:S(2)}) %all-to-all-start.2) | async-done | bytes 2228256 | tf_op jit(solution)/shard_map/all_to_all | solution.py:112
  136.9 2.6 %copy.66 = f32[16,128,128]{1,2,0:T(8,128)} copy(f32[16,128,128]{2,1,0:T(8,128)} %slice.198) | data formatting | bytes 2097152
  140.3 5.4 %bitcast_select_fusion.1 = (f32[16,128,128]{2,1,0:T(8,128)}, f32[16,128,128]{2,1,0:T(8,128)}, f32[16,128,128]{2,1,0:T(8,128)}, f32[16,128,128]{2,1,0:T(8,128)}, ...) fusion(f32[16,128,128]{1,2,0:T(8,128)} %copy.66, ...), kind=kLoop, calls=%fused_computation.21 | loop fusion | flops 1572864 | bytes 13697024 | tf_op jit(solution)/shard_map/jit(_where)/select_n | solution.py:37
  147.4 2.6 %copy.67 = f32[16,128,128]{1,2,0:T(8,128)} copy(f32[16,128,128]{2,1,0:T(8,128)} %get-tuple-element.33) | data formatting | bytes 2097152
  150.0 3.6 %fusion.7 = f32[16,256,256]{2,1,0:T(8,128)S(1)} fusion(f32[16,128,128]{2,1,0:T(8,128)} %get-tuple-element.46, f32[16,128,128]{2,1,0:T(8,128)S(1)} %copy.56, f32[16,128,128]{2,1,0:T(8,128)S(1)} %copy-done.2, f32[16,128,128]{2,1,0:T(8,128)} %get-tuple-element.47, f32[256,256]{1,0:T(8,128)S(1)} %fusion.10), kind=kOutput, calls=%fused_computation.31 | convolution fusion | flops 1613758464 | bytes 8650752 | tf_op jit(solution)/shard_map/wjb,bi->wji/dot_general | solution.py:120
  155.9 6.8 %collective-permute-start.3 = (f32[256,256]{1,0:T(8,128)S(1)}, f32[256,256]{1,0:T(8,128)S(1)}, u32[]{:S(2)}, u32[]{:S(2)}) collective-permute-start(f32[256,256]{1,0:T(8,128)S(1)} %convolution_bitcast_fusion.2), channel_id=1, source_target_pairs={{0,16},{16,0},{1,17},{17,1},{2,18},{18,2},{3,19},{19,3},{4,20},{20... | collective-permute-start | bytes 786440 | tf_op jit(solution)/shard_map/ppermute | solution.py:125
  170.3 3.6 %fusion.6 = f32[16,256,256]{2,1,0:T(8,128)S(1)} fusion(f32[16,128,128]{2,1,0:T(8,128)} %get-tuple-element.46, f32[16,128,128]{2,1,0:T(8,128)S(1)} %copy.56, f32[16,128,128]{2,1,0:T(8,128)S(1)} %copy-done.2, f32[16,128,128]{2,1,0:T(8,128)} %get-tuple-element.47, f32[256,256]{1,0:T(8,128)S(1)} %divide_select_fusion.1), kind=kOutput, calls=%fused_computation.30 | convolution fusion | flops 1613758464 | bytes 8650752 | tf_op jit(solution)/shard_map/wjb,bi->wji/dot_general | solution.py:120
  180.3 2.7 %multiply_reduce_fusion = (f32[]{:T(128)}, f32[256,256]{1,0:T(8,128)S(1)}) fusion(f32[]{:T(128)} %get-tuple-element.7, f32[256,256]{1,0:T(8,128)S(1)} %divide_select_fusion.1, f32[]{:T(128)} %get-tuple-element.6, f32[]{:T(128)} %sqrt.31, f32[256,256]{1,0:T(8,128)S(1)} %get-tuple-element.17, f32[]{:T(128)} %get-tuple-element.16, f32[]{:T(128)S(6)} %select_n.230, ...), kind=kLoop, calls=%fused_computation.47 | loop fusion | flops 917503 | bytes 1049113 | tf_op jit(solution)/shard_map/reduce_sum | solution.py:140
  183.8 3.6 %fusion.5 = f32[16,256,256]{2,1,0:T(8,128)S(1)} fusion(f32[16,128,128]{2,1,0:T(8,128)} %get-tuple-element.46, f32[16,128,128]{2,1,0:T(8,128)S(1)} %copy.56, f32[16,128,128]{2,1,0:T(8,128)S(1)} %copy-done.2, f32[16,128,128]{2,1,0:T(8,128)} %get-tuple-element.47, f32[256,256]{1,0:T(8,128)S(1)} %get-tuple-element.15, f32[]{:T(128)S(6)} %select_n.251, pred[]{:T(512)S(6)} %gt.28), kind=kOutput, calls=%fused_computation.29 | convolution fusion | flops 1613889536 | bytes 8650757 | tf_op jit(solution)/shard_map/wjb,bi->wji/dot_general | solution.py:120
  187.4 2.9 %fusion.8 = f32[]{:T(128)} fusion(f32[16,256,256]{2,1,0:T(8,128)S(1)} %fusion.5, f32[16,128,128]{2,1,0:T(8,128)S(1)} %copy-done.14, f32[16,128,128]{2,1,0:T(8,128)S(1)} %bitcast.179, f32[16,128,128]{2,1,0:T(8,128)S(1)} %copy-done.5, f32[16,128,128]{2,1,0:T(8,128)S(1)} %copy-done.11, f32[256,256]{1,0:T(8,128)S(1)} %get-tuple-element.15, f32[]{:T(128)S(6)} %select_n.251, ...), kind=kOutput, calls=%fused_computation.32 | convolution fusion | flops 1614020608 | bytes 8650761 | tf_op jit(solution)/shard_map/wja,wai->ji/dot_general | solution.py:121
  193.1 5.2 %all-to-all-start.3 = ((f32[128,1,8]{2,1,0:T(1,128)}), f32[128,1,8]{2,1,0:T(1,128)S(1)}, u32[]{:S(2)}, u32[]{:S(2)}) async-start(f32[128,1,8]{2,1,0:T(1,128)} %broadcast_in_dim.146), calls=%async_computation.3 | async-start | bytes 131072 | tf_op jit(solution)/shard_map/all_to_all | solution.py:152
  199.0 8.7 %all-to-all-done.3 = f32[128,1,8]{2,1,0:T(1,128)S(1)} async-done(((f32[128,1,8]{2,1,0:T(1,128)}), f32[128,1,8]{2,1,0:T(1,128)S(1)}, u32[]{:S(2)}, u32[]{:S(2)}) %all-to-all-start.3) | async-done | bytes 4128 | tf_op jit(solution)/shard_map/all_to_all | solution.py:152
  207.7 3.5 %all-to-all-start.4 = ((f32[16,16,256]{2,1,0:T(8,128)}), f32[16,16,256]{2,1,0:T(8,128)S(1)}, u32[]{:S(2)}, u32[]{:S(2)}) async-start(f32[16,16,256]{2,1,0:T(8,128)} %bitcast.45), calls=%async_computation.4 | async-start | bytes 524288 | tf_op jit(solution)/shard_map/all_to_all | solution.py:144
  (130 shorter events, 46.8 us)
Async XLA Ops:
  2.5 3.1 %collective-permute-start.2 = (f32[4,136,256]{2,1,0:T(8,128)S(1)}, f32[4,136,256]{2,1,0:T(8,128)S(1)}, u32[]{:S(2)}, u32[]{:S(2)}) collective-permute-start(f32[4,136,256]{2,1,0:T(8,128)S(1)} %select_maximum_fusion.1), channel_id=1, source_target_pairs={{0,16},{16,0},{1,17},{17,1},{2,18},{18,2},{3,19},{19,3},{4,20},{20... | collective-permute-start | bytes 1671176 | tf_op jit(solution)/shard_map/ppermute | solution.py:102
  8.2 5.0 %copy-start.16 = (s32[8,2]{0,1:T(2,128)S(1)}, s32[8,2]{0,1:T(2,128)}, u32[]{:S(2)}) copy-start(s32[8,2]{0,1:T(2,128)} %param.13) | copy-start | bytes 196
  8.2 5.0 %copy-start.17 = (s32[8]{0:T(128)S(1)}, s32[8]{0:T(128)}, u32[]{:S(2)}) copy-start(s32[8]{0:T(128)} %param.12) | copy-start | bytes 100
  8.2 5.5 %copy-start.15 = (f32[8,256,16]{1,2,0:T(8,128)S(1)}, f32[8,256,16]{1,2,0:T(8,128)}, u32[]{:S(2)}) copy-start(f32[8,256,16]{1,2,0:T(8,128)} %param.8) | copy-start | bytes 393220
  8.2 56.6 %all-to-all-start.1 = ((f32[4,8,136,256]{3,2,1,0:T(8,128)}), f32[4,8,136,256]{3,2,1,0:T(8,128)}, u32[]{:S(2)}, u32[]{:S(2)}) async-start(f32[4,8,136,256]{3,2,1,0:T(8,128)} %stack.56), calls=%async_computation.1 | async-start | bytes 8912896 | tf_op jit(solution)/shard_map/all_to_all | solution.py:104
  13.3 2.4 %collective-permute-start = (s32[8,3]{0,1:T(4,128)S(1)}, s32[8,3]{0,1:T(4,128)S(1)}, u32[]{:S(2)}, u32[]{:S(2)}) collective-permute-start(s32[8,3]{0,1:T(4,128)S(1)} %pad_add_fusion), channel_id=1, source_target_pairs={{0,16},{16,0},{1,17},{17,1},{2,18},{18,2},{3,19},{19,3},{4,20},{20... | collective-permute-start | bytes 296 | tf_op jit(solution)/shard_map/ppermute | solution.py:95
  13.7 7.9 %collective-permute-start.1 = (f32[8,16,256]{2,1,0:T(8,128)S(1)}, f32[8,16,256]{2,1,0:T(8,128)S(1)}, u32[]{:S(2)}, u32[]{:S(2)}) collective-permute-start(f32[8,16,256]{2,1,0:T(8,128)S(1)} %bitcast.180), channel_id=1, source_target_pairs={{0,16},{16,0},{1,17},{17,1},{2,18},{18,2},{3,19},{19,3},{4,20},{20... | collective-permute-start | bytes 393224 | tf_op jit(solution)/shard_map/ppermute | solution.py:96
  21.7 50.7 %copy-start.18 = (s32[64]{0:T(128)S(1)}, s32[64]{0:T(128)}, u32[]{:S(2)}) copy-start(s32[64]{0:T(128)} %param.11) | copy-start | bytes 772
  64.8 38.0 %all-to-all-start = ((f32[16,152,256]{2,1,0:T(8,128)}), f32[16,152,256]{2,1,0:T(8,128)S(1)}, u32[]{:S(2)}, u32[]{:S(2)}) async-start(f32[16,152,256]{2,1,0:T(8,128)} %fusion), calls=%async_computation | async-start | bytes 4980736 | tf_op jit(solution)/shard_map/all_to_all | solution.py:109
  76.8 34.1 %copy-start = (s32[32]{0:T(128)S(1)}, s32[32]{0:T(128)}, u32[]{:S(2)}) copy-start(s32[32]{0:T(128)} %param.14) | copy-start | bytes 388
  76.8 37.2 %copy-start.1 = (s32[8]{0:T(128)S(1)}, s32[8]{0:T(128)}, u32[]{:S(2)}) copy-start(s32[8]{0:T(128)} %param.15) | copy-start | bytes 100
  102.8 31.8 %all-to-all-start.2 = ((f32[16,136,256]{2,1,0:T(8,128)}), f32[16,136,256]{2,1,0:T(8,128)}, u32[]{:S(2)}, u32[]{:S(2)}) async-start(f32[16,136,256]{2,1,0:T(8,128)} %broadcast_select_fusion), calls=%async_computation.2 | async-start | bytes 4456448 | tf_op jit(solution)/shard_map/all_to_all | solution.py:112
  145.8 4.2 %copy-start.2 = (f32[16,128,128]{2,1,0:T(8,128)S(1)}, f32[16,128,128]{2,1,0:T(8,128)}, u32[]{:S(2)}) copy-start(f32[16,128,128]{2,1,0:T(8,128)} %get-tuple-element.44) | copy-start | bytes 3145732
  150.0 3.7 %copy-start.9 = (f32[16,128,128]{2,1,0:T(8,128)S(1)}, f32[16,128,128]{2,1,0:T(8,128)}, u32[]{:S(2)}) copy-start(f32[16,128,128]{2,1,0:T(8,128)} %get-tuple-element.27) | copy-start | bytes 3145732
  150.0 3.7 %copy-start.12 = (f32[16,128,128]{2,1,0:T(8,128)S(1)}, f32[16,128,128]{2,1,0:T(8,128)}, u32[]{:S(2)}) copy-start(f32[16,128,128]{2,1,0:T(8,128)} %get-tuple-element.28) | copy-start | bytes 3145732
  155.9 8.0 %collective-permute-start.3 = (f32[256,256]{1,0:T(8,128)S(1)}, f32[256,256]{1,0:T(8,128)S(1)}, u32[]{:S(2)}, u32[]{:S(2)}) collective-permute-start(f32[256,256]{1,0:T(8,128)S(1)} %convolution_bitcast_fusion.2), channel_id=1, source_target_pairs={{0,16},{16,0},{1,17},{17,1},{2,18},{18,2},{3,19},{19,3},{4,20},{20... | collective-permute-start | bytes 786440 | tf_op jit(solution)/shard_map/ppermute | solution.py:125
  170.3 3.7 %copy-start.4 = (f32[16,128,128]{2,1,0:T(8,128)S(1)}, f32[16,128,128]{2,1,0:T(8,128)}, u32[]{:S(2)}) copy-start(f32[16,128,128]{2,1,0:T(8,128)} %get-tuple-element.33) | copy-start | bytes 3145732
  170.3 3.7 %copy-start.7 = (f32[16,128,128]{1,2,0:T(8,128)S(1)}, f32[16,128,128]{1,2,0:T(8,128)}, u32[]{:S(2)}) copy-start(f32[16,128,128]{1,2,0:T(8,128)} %copy.67) | copy-start | bytes 3145732
  170.3 3.7 %copy-start.10 = (f32[16,128,128]{2,1,0:T(8,128)S(1)}, f32[16,128,128]{2,1,0:T(8,128)}, u32[]{:S(2)}) copy-start(f32[16,128,128]{2,1,0:T(8,128)} %get-tuple-element.27) | copy-start | bytes 3145732
  170.3 3.7 %copy-start.13 = (f32[16,128,128]{2,1,0:T(8,128)S(1)}, f32[16,128,128]{2,1,0:T(8,128)}, u32[]{:S(2)}) copy-start(f32[16,128,128]{2,1,0:T(8,128)} %get-tuple-element.28) | copy-start | bytes 3145732
  176.2 1.8 collective-permute-start.4
  193.1 14.6 %all-to-all-start.3 = ((f32[128,1,8]{2,1,0:T(1,128)}), f32[128,1,8]{2,1,0:T(1,128)S(1)}, u32[]{:S(2)}, u32[]{:S(2)}) async-start(f32[128,1,8]{2,1,0:T(1,128)} %broadcast_in_dim.146), calls=%async_computation.3 | async-start | bytes 131072 | tf_op jit(solution)/shard_map/all_to_all | solution.py:152
  207.7 17.8 %all-to-all-start.4 = ((f32[16,16,256]{2,1,0:T(8,128)}), f32[16,16,256]{2,1,0:T(8,128)S(1)}, u32[]{:S(2)}, u32[]{:S(2)}) async-start(f32[16,16,256]{2,1,0:T(8,128)} %bitcast.45), calls=%async_computation.4 | async-start | bytes 524288 | tf_op jit(solution)/shard_map/all_to_all | solution.py:144
  225.5 2.1 collective-permute-start.5
  (6 other events, 21.8 us)
